TPU v7x, 512 devices: a whole 4x4x16 slice. The times are simulated.
512 devices in a mesh: ctx: 32 (over x, y, core), mem: 16 (over z).
Axes of the slice: x: 4, y: 4, z: 16, core: 2. Of those that a mesh axis runs over, the one named last changes fastest.
Arguments:
- tokens: bfloat16 [131072, 1024], P(('ctx', 'mem')), may hold values from -36 to 36
- routes: int32 [131072, 2], P(('ctx', 'mem')), may hold values from 0 to 15, all different within a row; in each aligned block of 256 rows (0 to 255, 256 to 511, ...) at most 48 rows name the same one
- router: bfloat16 [1024, 16], replicated, may hold values from -0.1875 to 0.1875
- mem_weight: bfloat16 [16, 1024, 1536], P('mem'), may hold values from -0.1875 to 0.1875
- win_weight: bfloat16 [1024, 1536], P('mem'), may hold values from -3 to 3
Outputs:
- mixed: bfloat16 [131072, 512], P(('ctx', 'mem'))
Inputs may be any that keep to these rules, and one draw needn't show every extreme that they name: `routes`: each token names 2 different memories; the 256 tokens of one device name any one memory at most 48 times.
All inputs are finite; a program needn't handle non-finite values.
Results may differ from a plain program's by a relative error of at most 0.009.
Values may be sent and summed in bfloat16 or wider, within the bound.
A program may use at most 64 MiB of HBM per device.

v0:
```python
import jax
import jax.numpy as jnp
from jax import lax
from jax.sharding import PartitionSpec as P

HEADS = 4
HDIM = 128
WINDOW = 512


norm_eps = 1e-06


def passed_along(x, axis, by):
    devices = lax.axis_size(axis)
    pairs = [(i, i + by) for i in range(devices) if 0 <= i + by < devices]
    return lax.ppermute(x, axis, pairs)


def slot_table(route_rows, mems):
    matches = (route_rows[:, :, None] == jnp.arange(mems, dtype=jnp.int32)[None, None, :]).astype(
        jnp.int32
    )
    flat = matches.reshape(-1, mems)
    earlier = jnp.cumsum(flat, axis=0) - flat
    return jnp.sum(earlier * flat, axis=1).reshape(route_rows.shape)


def memory_local(slot_rows, positions, weight):
    projected = jnp.dot(slot_rows, weight, preferred_element_type=jnp.float32).astype(jnp.bfloat16)
    width = HEADS * HDIM
    causal = positions[None, :] <= positions[:, None]
    intra_list = []
    state_list = []
    for head_index in range(HEADS):
        column_start = head_index * HDIM
        queries = projected[:, column_start : column_start + HDIM]
        key_rows = projected[:, width + column_start : width + column_start + HDIM]
        value_rows = projected[:, 2 * width + column_start : 2 * width + column_start + HDIM]
        scores = lax.dot_general(
            queries, key_rows, (((1,), (1,)), ((), ())), preferred_element_type=jnp.float32
        )
        weights_low = jnp.where(causal, scores, 0.0).astype(jnp.bfloat16)
        intra_list.append(jnp.dot(weights_low, value_rows, preferred_element_type=jnp.float32))
        state_list.append(
            lax.dot_general(
                key_rows, value_rows, (((0,), (0,)), ((), ())), preferred_element_type=jnp.float32
            )
        )
    return (projected[:, :width], jnp.stack(intra_list), jnp.stack(state_list))


def memory_finish(queries, intra, prefix):
    outputs = []
    for head_index in range(HEADS):
        column_start = head_index * HDIM
        inter = jnp.dot(
            queries[:, column_start : column_start + HDIM],
            prefix[head_index].astype(jnp.bfloat16),
            preferred_element_type=jnp.float32,
        )
        summed = intra[head_index] + inter
        factor = lax.rsqrt(jnp.mean(summed * summed, axis=-1, keepdims=True) + norm_eps)
        outputs.append(summed * factor)
    return jnp.concatenate(outputs, axis=-1).astype(jnp.bfloat16)


def window_attend(queries, key_rows, value_rows, first_pos, count):
    distance = (
        jnp.arange(count, dtype=jnp.int32)[:, None]
        + 2 * count
        - jnp.arange(3 * count, dtype=jnp.int32)[None, :]
    )
    key_pos = first_pos - 2 * count + jnp.arange(3 * count, dtype=jnp.int32)
    allowed = (distance >= 0) & (distance < WINDOW) & (key_pos[None, :] >= 0)
    outputs = []
    for head_index in range(HEADS):
        column_start = head_index * HDIM
        scores = lax.dot_general(
            queries[:, column_start : column_start + HDIM],
            key_rows[:, column_start : column_start + HDIM],
            (((1,), (1,)), ((), ())),
            preferred_element_type=jnp.float32,
        ) * HDIM ** (-0.5)
        masked = jnp.where(allowed, scores, -1e30)
        highest = jnp.max(masked, axis=-1, keepdims=True)
        expo = jnp.exp(masked - highest)
        probs = (expo / jnp.sum(expo, axis=-1, keepdims=True)).astype(jnp.bfloat16)
        outputs.append(
            jnp.dot(
                probs,
                value_rows[:, column_start : column_start + HDIM],
                preferred_element_type=jnp.float32,
            )
        )
    return jnp.concatenate(outputs, axis=-1)


def project_window(rows, full_weight):
    return jnp.dot(rows, full_weight, preferred_element_type=jnp.float32).astype(jnp.bfloat16)


def shards(tokens, routes, router, mem_weight, win_weight):
    tok_dev = tokens.shape[0]
    mems = router.shape[1]
    n_mem = lax.axis_size("mem")
    capacity = 3 * tok_dev // mems
    width = HEADS * HDIM
    slots = slot_table(routes, mems)
    row_ids = jnp.broadcast_to(jnp.arange(tok_dev, dtype=jnp.int32)[:, None], routes.shape)
    values = jnp.broadcast_to(tokens[:, None, :], (tok_dev, routes.shape[1], tokens.shape[1]))
    dispatch = (
        jnp.zeros((mems, capacity, tokens.shape[1]), jnp.bfloat16).at[routes, slots].set(values)
    )
    found = jnp.full((mems, capacity), -1, jnp.int32).at[routes, slots].set(row_ids)
    arrived, arrived_ids = (
        lax.all_to_all(dispatch, "mem", split_axis=0, concat_axis=0, tiled=True),
        lax.all_to_all(found, "mem", split_axis=0, concat_axis=0, tiled=True),
    )
    positions = (jnp.arange(n_mem, dtype=jnp.int32)[:, None] * tok_dev + arrived_ids).reshape(-1)
    queries, intra, state = memory_local(
        arrived.reshape(-1, tokens.shape[1]), positions, mem_weight[0]
    )
    my_index = lax.axis_index("ctx")
    shard_states = lax.all_gather(state[None], "ctx", axis=0, tiled=True)
    indices = jnp.arange(shard_states.shape[0], dtype=jnp.int32)
    keep = (indices < my_index).astype(jnp.float32)
    prefix = jnp.einsum("s,shij->hij", keep, shard_states)
    finished = memory_finish(queries, intra, prefix).reshape(n_mem, capacity, width)
    returned = lax.all_to_all(finished, "mem", split_axis=0, concat_axis=0, tiled=True)
    picked = returned[routes, slots].astype(jnp.float32)
    logits = jnp.dot(tokens, router, preferred_element_type=jnp.float32)
    matches = (routes[:, :, None] == jnp.arange(mems, dtype=jnp.int32)[None, None, :]).astype(
        jnp.float32
    )
    chosen = jnp.sum(matches * logits[:, None, :], axis=-1)
    gates = jax.nn.sigmoid(chosen[:, 0] - chosen[:, 1])
    memory_part = gates[:, None] * picked[:, 0] + (1.0 - gates)[:, None] * picked[:, 1]
    full_weight = lax.all_gather(win_weight, "mem", axis=0, tiled=True)
    first_pos = lax.axis_index(("ctx", "mem")) * tok_dev
    projected = project_window(tokens, full_weight)
    own_keys = projected[:, width:]
    earlier_keys = [passed_along(own_keys, ("ctx", "mem"), offset) for offset in (2, 1)]
    key_block = jnp.concatenate(earlier_keys + [own_keys], axis=0)
    query_rows = projected[:, :width]
    window_part = window_attend(
        query_rows, key_block[:, :width], key_block[:, width:], first_pos, tok_dev
    )
    return (memory_part + window_part).astype(jnp.bfloat16)


def solution(mesh):
    return jax.shard_map(
        shards,
        mesh=mesh,
        in_specs=(
            P(("ctx", "mem"), None),
            P(("ctx", "mem"), None),
            P(),
            P("mem", None, None),
            P("mem", None),
        ),
        out_specs=P(("ctx", "mem"), None),
        check_vma=False,
    )
```

profile of v0, /device:TPU:7, one launch (start us, length us, event | category | flops | bytes accessed | tf_op | source)
XLA Modules:
  0.0 404.1 jit_solution(2668983449262850495)
XLA Ops:
  6.5 1.0 copy.48
  7.8 1.2 reduce-window.6
  9.5 0.7 fusion.97
  10.5 2.6 broadcast_in_dim.29
  13.2 2.3 reshape.163
  15.4 1.3 broadcast_in_dim.28
  16.8 73.0 %scatter_fusion.1 = bf16[16,48,1024]{2,1,0:T(8,128)(2,1)} fusion(bf16[16,48,1024]{2,1,0:T(8,128)(2,1)} %broadcast_in_dim.28, s32[512]{0:T(512)S(1)} %reshape.155, bf16[512,1024]{1,0:T(8,128)(2,1)} %reshape.163), kind=kCustom, calls=%fused_computation.2 | custom fusion | bytes 3149824 | tf_op jit(solution)/shard_map/scatter | solution.py:113
  89.8 15.0 %all-to-all-start.1 = ((bf16[16,48,1024]{2,1,0:T(8,128)(2,1)}), bf16[16,48,1024]{2,1,0:T(8,128)(2,1)}, u32[]{:S(2)}, u32[]{:S(2)}) async-start(bf16[16,48,1024]{2,1,0:T(8,128)(2,1)} %scatter_fusion.1), calls=%async_computation.1 | async-start | bytes 3145728 | tf_op jit(solution)/shard_map/all_to_all | solution.py:117
  104.8 0.7 all-gather.4.cloned.1.call-update
  105.6 80.7 %all-to-all-done.1 = bf16[16,48,1024]{2,1,0:T(8,128)(2,1)} async-done(((bf16[16,48,1024]{2,1,0:T(8,128)(2,1)}), bf16[16,48,1024]{2,1,0:T(8,128)(2,1)}, u32[]{:S(2)}, u32[]{:S(2)}) %all-to-all-start.1) | async-done | bytes 1572896 | tf_op jit(solution)/shard_map/all_to_all | solution.py:117
  186.2 4.2 %convolution_convert_fusion = bf16[768,1536]{1,0:T(8,128)(2,1)S(1)} fusion(bf16[768,1024]{1,0:T(8,128)(2,1)} %bitcast.5, bf16[1,1024,1536]{2,1,0:T(8,128)(2,1)S(1)} %copy-done), kind=kOutput, calls=%fused_computation.9 | convolution fusion | flops 2417098752 | bytes 7077888 | tf_op jit(solution)/shard_map/dot_general | solution.py:30
  191.2 0.7 copy-done.2
  192.2 0.7 pad_maximum_fusion.2
  193.0 0.6 broadcast_in_dim.25
  193.6 68.2 %scatter_fusion = s32[16,48]{1,0:T(8,128)} fusion(s32[16,48]{1,0:T(8,128)} %broadcast_in_dim.25, s32[512]{0:T(512)S(1)} %reshape.155, s32[512]{0:T(512)S(1)} %reshape.157), kind=kCustom, calls=%fused_computation.1 | custom fusion | bytes 10240 | tf_op jit(solution)/shard_map/scatter | solution.py:115
  261.9 11.5 %all-to-all-start = ((s32[16,1,48]{2,1,0:T(1,128)}), s32[16,1,48]{2,1,0:T(1,128)S(1)}, u32[]{:S(2)}, u32[]{:S(2)}) async-start(s32[16,1,48]{2,1,0:T(1,128)} %bitcast.4), calls=%async_computation | async-start | bytes 16384 | tf_op jit(solution)/shard_map/all_to_all | solution.py:118
  273.4 0.5 iota_add_fusion
  273.9 0.5 add_compare_fusion
  274.5 1.3 fusion.129
  275.7 0.6 select_reduce_fusion
  276.8 7.8 %all-to-all-done = s32[16,1,48]{2,1,0:T(1,128)S(1)} async-done(((s32[16,1,48]{2,1,0:T(1,128)}), s32[16,1,48]{2,1,0:T(1,128)S(1)}, u32[]{:S(2)}, u32[]{:S(2)}) %all-to-all-start) | async-done | bytes 3104 | tf_op jit(solution)/shard_map/all_to_all | solution.py:118
  284.6 0.6 broadcast.259
  285.2 0.7 reduce.5
  286.1 3.0 convolution_convert_fusion.1
  289.1 0.9 copy-done.1
  290.0 0.9 slice.196
  290.9 2.2 collective-permute-start
  293.1 2.4 collective-permute-start.1
  295.5 4.6 %fusion = f32[1,4,128,128]{3,0,2,1:T(1,128)S(1)} fusion(bf16[32,4,128,128]{3,2,1,0:T(8,128)(2,1)} %bitcast.87, s32[]{:T(128)S(6)} %axis_index.27), kind=kOutput, calls=%fused_computation.3 | convolution fusion | flops 4194336 | bytes 4456452 | tf_op jit(solution)/shard_map/s,shij->hij/dot_general | solution.py:128
  300.2 1.9 fusion.85
  302.0 1.9 fusion.61
  303.9 1.9 fusion.57
  305.8 1.9 fusion.53
  307.7 2.2 multiply_reduce_fusion.3
  309.9 3.4 multiply_reduce_fusion.2
  313.3 0.7 add_rsqrt_fusion.2
  314.0 3.5 multiply_reduce_fusion.1
  317.4 0.7 add_rsqrt_fusion.1
  318.1 3.5 multiply_reduce_fusion
  321.6 0.7 add_rsqrt_fusion
  322.5 1.2 multiply_convert_fusion.2
  323.7 1.2 multiply_convert_fusion.1
  324.8 1.2 multiply_convert_fusion
  326.0 1.0 pad_maximum_fusion.1
  327.0 9.3 %all-to-all-start.2 = ((bf16[16,48,512]{2,1,0:T(8,128)(2,1)}), bf16[16,48,512]{2,1,0:T(8,128)(2,1)}, u32[]{:S(2)}, u32[]{:S(2)}) async-start(bf16[16,48,512]{2,1,0:T(8,128)(2,1)} %pad_maximum_fusion.1), calls=%async_computation.2 | async-start | bytes 1572864 | tf_op jit(solution)/shard_map/all_to_all | solution.py:130
  336.4 1.5 pad_maximum_fusion
  337.9 1.3 fusion.112
  339.2 0.3 fusion.35
  339.5 1.3 fusion.111
  340.8 0.3 fusion.36
  341.1 1.3 fusion.110
  342.7 1.3 fusion.109
  344.3 0.4 fusion.41
  344.7 1.1 fusion.42
  345.8 1.1 fusion.43
  346.9 1.1 fusion.44
  347.9 27.4 %all-to-all-done.2 = bf16[16,48,512]{2,1,0:T(8,128)(2,1)} async-done(((bf16[16,48,512]{2,1,0:T(8,128)(2,1)}), bf16[16,48,512]{2,1,0:T(8,128)(2,1)}, u32[]{:S(2)}, u32[]{:S(2)}) %all-to-all-start.2) | async-done | bytes 786464 | tf_op jit(solution)/shard_map/all_to_all | solution.py:130
  375.3 9.6 %gather_fusion = bf16[512,512]{1,0:T(8,128)(2,1)} fusion(bf16[16,48,512]{2,1,0:T(8,128)(2,1)} %all-to-all-done.2, s32[512]{0:T(512)S(1)} %reshape.149), kind=kCustom, calls=%fused_computation | custom fusion | bytes 1052672 | tf_op jit(solution)/shard_map/gather | solution.py:131
  384.9 2.7 reshape.168
  387.6 3.5 fusion.108
  391.0 1.9 copy.63
  393.0 1.9 copy.64
  394.9 1.5 fusion.39
  396.4 0.8 copy.59
  (53 shorter events, 3.8 us)
Async XLA Ops:
  6.5 179.7 %copy-start = (bf16[1,1024,1536]{2,1,0:T(8,128)(2,1)S(1)}, bf16[1,1024,1536]{2,1,0:T(8,128)(2,1)}, u32[]{:S(2)}) copy-start(bf16[1,1024,1536]{2,1,0:T(8,128)(2,1)} %param.8) | copy-start | bytes 9437188
  89.8 96.4 %all-to-all-start.1 = ((bf16[16,48,1024]{2,1,0:T(8,128)(2,1)}), bf16[16,48,1024]{2,1,0:T(8,128)(2,1)}, u32[]{:S(2)}, u32[]{:S(2)}) async-start(bf16[16,48,1024]{2,1,0:T(8,128)(2,1)} %scatter_fusion.1), calls=%async_computation.1 | async-start | bytes 3145728 | tf_op jit(solution)/shard_map/all_to_all | solution.py:117
  104.8 181.3 %all-gather.4.cloned.1.call-start = ((), (), s32[]{:S(2)}) async-start(), calls=%async_computation.3 | async-start | bytes 3342336 | tf_op jit(solution)/shard_map/all_gather | solution.py:139
  105.5 190.0 %all-gather.6.cloned.1.call-start = ((), (), s32[]{:S(2)}) async-start(), calls=%async_computation.4 | async-start | bytes 4325376 | tf_op jit(solution)/shard_map/all_gather | solution.py:125
  190.4 1.5 copy-start.2
  193.6 80.8 %copy-start.3 = (bf16[1024,16]{0,1:T(8,128)(2,1)S(1)}, bf16[1024,16]{0,1:T(8,128)(2,1)}, u32[]{:S(2)}) copy-start(bf16[1024,16]{0,1:T(8,128)(2,1)} %param.7) | copy-start | bytes 98308
  193.6 82.1 %copy-start.4 = (s32[256,2]{0,1:T(2,128)S(1)}, s32[256,2]{0,1:T(2,128)}, u32[]{:S(2)}) copy-start(s32[256,2]{0,1:T(2,128)} %param.6) | copy-start | bytes 6148
  261.9 22.8 %all-to-all-start = ((s32[16,1,48]{2,1,0:T(1,128)}), s32[16,1,48]{2,1,0:T(1,128)S(1)}, u32[]{:S(2)}, u32[]{:S(2)}) async-start(s32[16,1,48]{2,1,0:T(1,128)} %bitcast.4), calls=%async_computation | async-start | bytes 16384 | tf_op jit(solution)/shard_map/all_to_all | solution.py:118
  286.0 28.0 %copy-start.6 = (s32[768]{0:T(1024)}, s32[768]{0:T(1024)S(1)}, u32[]{:S(2)}) copy-start(s32[768]{0:T(1024)S(1)} %add.120) | copy-start | bytes 9220
  289.1 0.9 copy-start.1
  290.9 45.5 %collective-permute-start = (bf16[256,1024]{1,0:T(8,128)(2,1)}, bf16[256,1024]{1,0:T(8,128)(2,1)}, u32[]{:S(2)}, u32[]{:S(2)}) collective-permute-start(bf16[256,1024]{1,0:T(8,128)(2,1)} %slice.196), channel_id=1, source_target_pairs={{0,2},{1,3},{2,4},{3,5},{4,6},{5,7},{6,8},{7,9},{8,10},{9,11},{10,... | collective-permute-start | bytes 1572872 | tf_op jit(solution)/shard_map/ppermute | solution.py:17
  293.1 43.3 %collective-permute-start.1 = (bf16[256,1024]{1,0:T(8,128)(2,1)}, bf16[256,1024]{1,0:T(8,128)(2,1)}, u32[]{:S(2)}, u32[]{:S(2)}) collective-permute-start(bf16[256,1024]{1,0:T(8,128)(2,1)} %slice.196), channel_id=1, source_target_pairs={{0,1},{1,2},{2,3},{3,4},{4,5},{5,6},{6,7},{7,8},{8,9},{9,10},{10,1... | collective-permute-start | bytes 1572872 | tf_op jit(solution)/shard_map/ppermute | solution.py:17
  322.5 13.8 %copy-start.5 = (f32[256,2]{0,1:T(2,128)S(1)}, f32[256,2]{0,1:T(2,128)}, u32[]{:S(2)}) copy-start(f32[256,2]{0,1:T(2,128)} %select_reduce_fusion) | copy-start | bytes 6148
  327.0 10.9 %copy-start.7 = (pred[768]{0:T(1024)(128)(4,1)S(1)}, pred[768]{0:T(1024)(128)(4,1)}, u32[]{:S(2)}) copy-start(pred[768]{0:T(1024)(128)(4,1)} %add_compare_fusion) | copy-start | bytes 2308
  327.0 10.9 %copy-start.8 = (s32[256]{0:T(256)S(1)}, s32[256]{0:T(256)}, u32[]{:S(2)}) copy-start(s32[256]{0:T(256)} %iota_add_fusion) | copy-start | bytes 3076
  327.0 48.3 %all-to-all-start.2 = ((bf16[16,48,512]{2,1,0:T(8,128)(2,1)}), bf16[16,48,512]{2,1,0:T(8,128)(2,1)}, u32[]{:S(2)}, u32[]{:S(2)}) async-start(bf16[16,48,512]{2,1,0:T(8,128)(2,1)} %pad_maximum_fusion.1), calls=%async_computation.2 | async-start | bytes 1572864 | tf_op jit(solution)/shard_map/all_to_all | solution.py:130
Sparse Core Ops, SparseCore 0:
  107.7 110.3 all-gather.3
  221.2 63.4 all-gather.5
where the time goes:
time: 410 us; the launch traced here: 404 us
  local copies, waits for them, and re-layouts  174 us (42%)
  waiting for transfers between devices  117 us (29%)
  matrix products  43.1 us (11%)
  starting transfers between devices  40.6 us (10%)
  other arithmetic  15.9 us (4%)
  between operations  13.7 us (3%)
    all_to_all x1, waiting for transfers between devices, shards(): lax.all_to_all(dispatch, 'mem', split_axis=0, concat_axis=0, tiled=True)  80.7 us
    scatter x1, local copies, waits for them, and re-layouts, shards(): jnp.zeros((mems, capacity, tokens.shape[1]), jnp.bfloat16).at[routes, slots]  73 us
    scatter x1, local copies, waits for them, and re-layouts, shards(): jnp.full((mems, capacity), -1, jnp.int32).at[routes, slots].set(row_ids)  68.2 us
    all_to_all x1, waiting for transfers between devices, shards(): lax.all_to_all(finished, 'mem', split_axis=0, concat_axis=0, tiled=True)  27.4 us
    all_to_all x1, starting transfers between devices, shards(): lax.all_to_all(dispatch, 'mem', split_axis=0, concat_axis=0, tiled=True)  15 us
    dot_general x4, matrix products, memory_local(): jnp.dot(weights_low, value_rows, preferred_element_type=jnp.float32)  12.6 us
    all_to_all x1, starting transfers between devices, shards(): lax.all_to_all(found, 'mem', split_axis=0, concat_axis=0, tiled=True)  11.5 us
    gather x1, local copies, waits for them, and re-layouts, shards(): picked = returned[routes, slots].astype(jnp.float32)  9.59 us
  transfers between devices with their start and end apart: 7, of which 3 were waited for; matrix products, arithmetic and copies ran while one was open for 31% of the time, Pallas kernels for 0%

commit v1 on v0

v1 whole, which is shorter than its diff:
```python
import functools

import jax
import jax.numpy as jnp
from jax import lax
from jax.experimental import pallas as pl
from jax.experimental.pallas import tpu as pltpu
from jax.sharding import PartitionSpec as P

MESH = pl.DeviceIdType.MESH
HEADS = 4
HDIM = 128
WIDTH = HEADS * HDIM
WINDOW = 512
TOK = 256
MEMS = 16
CAP = 48
ROWS = MEMS * CAP
DEPTH = 1024
COLS = 3 * WIDTH
CHIPS = 16
WIN_TILES = COLS // 128
norm_eps = 1e-06
bf16 = jnp.bfloat16
f32 = jnp.float32


def mm(a, b):
    return jnp.dot(a, b, preferred_element_type=f32)


def mm_nt(a, b):
    return lax.dot_general(a, b, (((1,), (1,)), ((), ())), preferred_element_type=f32)


def mm_tn(a, b):
    return lax.dot_general(a, b, (((0,), (0,)), ((), ())), preferred_element_type=f32)


def remote(src, dst, send, recv, device):
    return pltpu.make_async_remote_copy(
        src_ref=src, dst_ref=dst, send_sem=send, recv_sem=recv, device_id=device, device_id_type=MESH
    )


def cols(start, size=128):
    return pl.ds(pl.multiple_of(start, 128), size)


def rows_of(j, size=CAP):
    return pl.ds(pl.multiple_of(j * size, 16), size)


def loop(low, high, body):
    def step(n, carry):
        body(n)
        return carry

    lax.fori_loop(low, high, step, 0)


def kernel(
    tok, routes, router, w_hbm, win, out,
    pick0, pick1, sbuf, rbuf, wmem, wz, wwin, proj, intra, winq, kv,
    st_own, st_part, st_send, st_all, pre_send, pre_part, pre, fbuf, ret, wout, gcol,
    s_disp, r_disp, s_ret, r_ret, s_wz, r_wz, s_wp, r_wp, s_st, r_st, one_s, one_r, local,
):
    ctx = lax.axis_index("ctx")
    me = lax.axis_index("mem")
    chip = ctx // 2
    core = ctx % 2
    blk = ctx
    seq = blk * MEMS + me

    def member(j):
        return {"ctx": ctx, "mem": j}

    def peer(j):
        return {"ctx": 2 * j + core, "mem": me}

    def at_seq(n):
        n = (n + 32 * MEMS) % (32 * MEMS)
        return {"ctx": n // MEMS, "mem": n % MEMS}

    partner = {"ctx": 2 * chip + 1 - core, "mem": me}

    w_copy = pltpu.make_async_copy(w_hbm.at[0], wmem, local.at[0])
    w_copy.start()

    barrier = pltpu.get_barrier_semaphore()

    def greet(off):
        pl.semaphore_signal(barrier, inc=1, device_id=member((me + off) % MEMS), device_id_type=MESH)
        pl.semaphore_signal(barrier, inc=1, device_id=peer((chip + off) % CHIPS), device_id_type=MESH)

    loop(1, 16, greet)
    pl.semaphore_signal(barrier, inc=1, device_id=partner, device_id_type=MESH)
    for off in (-2, -1, 1, 2):
        pl.semaphore_signal(barrier, inc=1, device_id=at_seq(seq + off), device_id_type=MESH)

    first, second = routes[0:1, :], routes[1:2, :]
    mem_ids = lax.broadcasted_iota(jnp.int32, (MEMS, TOK), 0)
    match0 = jnp.where(mem_ids == first, 1.0, 0.0).astype(f32)
    match1 = jnp.where(mem_ids == second, 1.0, 0.0).astype(f32)
    earlier = jnp.where(
        lax.broadcasted_iota(jnp.int32, (TOK, TOK), 0) < lax.broadcasted_iota(jnp.int32, (TOK, TOK), 1), 1.0, 0.0
    ).astype(bf16)
    counts = mm((match0 + match1).astype(bf16), earlier)
    slot0 = jnp.sum(match0 * counts, axis=0, keepdims=True).astype(jnp.int32)
    slot1 = jnp.sum(match1 * counts, axis=0, keepdims=True).astype(jnp.int32)
    row_ids = lax.broadcasted_iota(jnp.int32, (ROWS, TOK), 0)
    is0 = jnp.where(row_ids == first * CAP + slot0, 1.0, 0.0).astype(f32)
    is1 = jnp.where(row_ids == second * CAP + slot1, 1.0, 0.0).astype(f32)
    pick0[...] = is0.astype(bf16)
    pick1[...] = is1.astype(bf16)
    picked = (is0 + is1).astype(bf16)
    for n in range(2):
        sbuf[:, n * 512 : (n + 1) * 512] = mm(picked, tok[:, n * 512 : (n + 1) * 512]).astype(bf16)

    logits = mm_nt(router[...], tok[...])
    diff = jnp.sum((match0 - match1) * logits, axis=0, keepdims=True)
    gate = jax.nn.sigmoid(diff)
    gcol[...] = jnp.transpose(jnp.broadcast_to(gate, (128, TOK)))

    pl.semaphore_wait(barrier, 15 + 15 + 1 + 4)

    half = pl.ds(pl.multiple_of(core * 32, 32), 32)

    def wz_copy(j, slot, device):
        return remote(win.at[half, cols(chip * 128)], wz.at[slot], s_wz.at[j], r_wz.at[slot], device)

    @pl.when(chip < WIN_TILES)
    def _():
        def send(off):
            j = (me + off) % MEMS
            wz_copy(j, me, member(j)).start()

        loop(1, 16, send)
        pltpu.make_async_copy(win.at[half, cols(chip * 128)], wz.at[me], local.at[1]).start()

    def disp_copy(j, slot, device):
        return remote(sbuf.at[rows_of(j)], rbuf.at[rows_of(slot)], s_disp.at[j], r_disp.at[slot], device)

    def send_rows(n):
        near = 8 - (n + 1) // 2
        off = jnp.where(n % 2 == 0, near, MEMS - near)
        j = (me + off) % MEMS
        disp_copy(j, me, member(j)).start()

    loop(0, 15, send_rows)
    own_rows = pltpu.make_async_copy(sbuf.at[rows_of(me)], rbuf.at[rows_of(me)], local.at[2])
    own_rows.start()

    def wp_block(j, b):
        return wwin.at[:, pl.ds(pl.multiple_of(b * 32, 32), 32), cols(j * 128)]

    @pl.when(chip < WIN_TILES)
    def _():
        def arrive(off):
            j = (me + off) % MEMS
            wz_copy(j, j, member(j)).wait_recv()

        loop(1, 16, arrive)
        pltpu.make_async_copy(win.at[half, cols(chip * 128)], wz.at[me], local.at[1]).wait()

        def send(off):
            j = (chip + off) % CHIPS
            remote(wz, wp_block(chip, core), s_wp.at[j], r_wp.at[chip], peer(j)).start()

        loop(1, 16, send)
        pltpu.make_async_copy(wz, wp_block(chip, core), local.at[1]).start()

    def wp_arrive(j):
        @pl.when(j != chip)
        def _():
            remote(wz, wp_block(j, core), s_wp.at[j], r_wp.at[j], partner).wait_recv()

        @pl.when(j == chip)
        def _():
            pltpu.make_async_copy(wz, wp_block(j, core), local.at[1]).wait()

    loop(0, WIN_TILES, wp_arrive)
    wc_copy = remote(wwin.at[:, half, :], wwin.at[:, half, :], one_s.at[0], one_r.at[0], partner)
    wc_copy.start()
    wc_copy.wait_recv()

    def win_project(n):
        w = wwin[:, :, cols(n * 256, 256)].reshape(DEPTH, 256)
        res = mm(tok[...], w).astype(bf16)

        @pl.when(n < 2)
        def _():
            winq[:, cols(n * 256, 256)] = res

        @pl.when(n >= 2)
        def _():
            kv[pl.ds(2 * TOK, TOK), cols((n - 2) * 256, 256)] = res

    loop(0, 6, win_project)

    w_copy.wait()

    def project(g):
        def arrive(k):
            j = 4 * g + k

            @pl.when(j != me)
            def _():
                disp_copy(j, j, partner).wait_recv()

            @pl.when(j == me)
            def _():
                own_rows.wait()

        loop(0, 4, arrive)

        def tile(n):
            proj[rows_of(g, 192), cols(n * 512, 512)] = mm(rbuf[rows_of(g, 192), :], wmem[:, cols(n * 512, 512)]).astype(
                bf16
            )

        loop(0, 3, tile)

    loop(0, 4, project)

    def kv_copy(n):
        return remote(
            kv.at[pl.ds(2 * TOK, TOK)],
            kv.at[pl.ds((2 - n) * TOK, TOK)],
            one_s.at[n],
            one_r.at[n],
            at_seq(seq + n),
        )

    kv_copy(1).start()
    kv_copy(2).start()

    def state(h):
        st_own[h] = mm_tn(proj[:, cols(WIDTH + h * HDIM)], proj[:, cols(2 * WIDTH + h * HDIM)])

    loop(0, HEADS, state)
    st_copy = remote(st_own, st_part, one_s.at[3], one_r.at[3], partner)
    st_copy.start()

    def attend(h):
        q = proj[:, cols(h * HDIM)]
        k = proj[:, cols(WIDTH + h * HDIM)]
        v = proj[:, cols(2 * WIDTH + h * HDIM)]
        keep = lax.broadcasted_iota(jnp.int32, (256, 256), 1) <= lax.broadcasted_iota(jnp.int32, (256, 256), 0)
        for b in range(3):
            lo, hi = b * 256, (b + 1) * 256
            scores = jnp.where(keep, mm_nt(q[lo:hi], k[lo:hi]), 0.0).astype(bf16)
            total = mm(scores, v[lo:hi])
            if b:
                total = total + mm(mm_nt(q[lo:hi], k[:lo]).astype(bf16), v[:lo])
            intra[lo:hi, cols(h * HDIM)] = total

    st_copy.wait()
    mine = pl.ds(2 * core, 2)
    st_send[...] = (st_own[mine] + st_part[mine]).astype(bf16)

    def st_copy_of(j, slot, device):
        return remote(st_send, st_all.at[slot], s_st.at[j], r_st.at[slot], device)

    def st_out(j):
        st_copy_of(j, chip, peer(j)).start()

    loop(chip + 1, CHIPS, st_out)
    loop(0, HEADS, attend)
    pre_send[...] = jnp.zeros_like(pre_send)

    def st_in(j):
        st_copy_of(j, j, partner).wait_recv()
        pre_send[...] += st_all[j].astype(f32)

    loop(0, chip, st_in)
    pre_copy = remote(pre_send, pre_part, one_s.at[4], one_r.at[4], partner)
    pre_copy.start()
    pre_copy.wait_recv()

    for h in range(HEADS):
        lower = core == h // 2

        @pl.when(lower)
        def _():
            st_own[h] = pre_send[h % 2]

        @pl.when(jnp.logical_not(lower))
        def _():
            st_own[h] = pre_part[h % 2]

    @pl.when(core == 0)
    def _():
        pre[...] = st_own[...].astype(bf16)

    @pl.when(core == 1)
    def _():
        pre[...] = (st_own[...] + st_part[...]).astype(bf16)

    def finish(h):
        summed = intra[:, cols(h * HDIM)] + mm(proj[:, cols(h * HDIM)], pre[h])
        factor = lax.rsqrt(jnp.mean(summed * summed, axis=-1, keepdims=True) + norm_eps)
        fbuf[:, cols(h * HDIM)] = (summed * factor).astype(bf16)

    loop(0, HEADS, finish)

    def ret_copy(j, slot, device):
        return remote(fbuf.at[rows_of(j)], ret.at[rows_of(slot)], s_ret.at[j], r_ret.at[slot], device)

    def send_back(n):
        near = 8 - (n + 1) // 2
        off = jnp.where(n % 2 == 0, near, MEMS - near)
        j = (me + off) % MEMS
        ret_copy(j, me, member(j)).start()

    loop(0, 15, send_back)
    own_ret = pltpu.make_async_copy(fbuf.at[rows_of(me)], ret.at[rows_of(me)], local.at[3])
    own_ret.start()

    kv_copy(1).wait_recv()
    kv_copy(2).wait_recv()
    first_pos = seq * TOK

    def window(h):
        for b in range(2):
            lo = b * 128
            q = winq[lo : lo + 128, cols(h * HDIM)]
            k = kv[lo : lo + 640, cols(h * HDIM)]
            v = kv[lo : lo + 640, cols(WIDTH + h * HDIM)]
            scores = mm_nt(q, k) * HDIM ** (-0.5)
            key = lax.broadcasted_iota(jnp.int32, (128, 640), 1)
            distance = lax.broadcasted_iota(jnp.int32, (128, 640), 0) + 2 * TOK - key
            allowed = (distance >= 0) & (distance < WINDOW) & (key + lo + first_pos - 2 * TOK >= 0)
            masked = jnp.where(allowed, scores, -1e30)
            expo = jnp.exp(masked - jnp.max(masked, axis=-1, keepdims=True))
            probs = (expo / jnp.sum(expo, axis=-1, keepdims=True)).astype(bf16)
            wout[lo : lo + 128, cols(h * HDIM)] = mm(probs, v)

    loop(0, HEADS, window)

    def ret_in(off):
        j = (me + off) % MEMS
        ret_copy(j, j, member(j)).wait_recv()

    loop(1, 16, ret_in)
    own_ret.wait()

    def combine(h):
        res = ret[:, cols(h * HDIM)]
        g = gcol[...]
        part = g * mm_tn(pick0[...], res) + (1.0 - g) * mm_tn(pick1[...], res)
        out[:, cols(h * HDIM)] = (part + wout[:, cols(h * HDIM)]).astype(bf16)

    loop(0, HEADS, combine)

    def left(off):
        j = (me + off) % MEMS
        disp_copy(j, me, member(j)).wait_send()
        ret_copy(j, me, member(j)).wait_send()

        @pl.when(chip < WIN_TILES)
        def _():
            wz_copy(j, me, member(j)).wait_send()
            i = (chip + off) % CHIPS
            remote(wz, wp_block(chip, core), s_wp.at[i], r_wp.at[chip], peer(i)).wait_send()

    loop(1, 16, left)

    def st_left(j):
        st_copy_of(j, chip, peer(j)).wait_send()

    loop(chip + 1, CHIPS, st_left)
    wc_copy.wait_send()
    kv_copy(1).wait_send()
    kv_copy(2).wait_send()
    pre_copy.wait_send()


def shards(tokens, routes, router, mem_weight, win_weight):
    vmem = pl.BlockSpec(memory_space=pltpu.VMEM)
    dma = pltpu.SemaphoreType.DMA
    return pl.pallas_call(
        kernel,
        out_shape=jax.ShapeDtypeStruct((TOK, WIDTH), bf16),
        in_specs=[vmem, vmem, vmem, pl.BlockSpec(memory_space=pl.ANY), vmem],
        out_specs=vmem,
        scratch_shapes=[
            pltpu.VMEM((ROWS, TOK), bf16),
            pltpu.VMEM((ROWS, TOK), bf16),
            pltpu.VMEM((ROWS, DEPTH), bf16),
            pltpu.VMEM((ROWS, DEPTH), bf16),
            pltpu.VMEM((DEPTH, COLS), bf16),
            pltpu.VMEM((MEMS, 32, 128), bf16),
            pltpu.VMEM((MEMS, 64, COLS), bf16),
            pltpu.VMEM((ROWS, COLS), bf16),
            pltpu.VMEM((ROWS, WIDTH), f32),
            pltpu.VMEM((TOK, WIDTH), bf16),
            pltpu.VMEM((3 * TOK, 2 * WIDTH), bf16),
            pltpu.VMEM((HEADS, HDIM, HDIM), f32),
            pltpu.VMEM((HEADS, HDIM, HDIM), f32),
            pltpu.VMEM((2, HDIM, HDIM), bf16),
            pltpu.VMEM((CHIPS, 2, HDIM, HDIM), bf16),
            pltpu.VMEM((2, HDIM, HDIM), f32),
            pltpu.VMEM((2, HDIM, HDIM), f32),
            pltpu.VMEM((HEADS, HDIM, HDIM), bf16),
            pltpu.VMEM((ROWS, WIDTH), bf16),
            pltpu.VMEM((ROWS, WIDTH), bf16),
            pltpu.VMEM((TOK, WIDTH), f32),
            pltpu.VMEM((TOK, 128), f32),
        ]
        + [dma((16,))] * 10
        + [dma((5,)), dma((5,)), dma((4,))],
        compiler_params=pltpu.CompilerParams(
            collective_id=0, has_side_effects=True, vmem_limit_bytes=56 * 1024 * 1024
        ),
    )(tokens, routes.T, router.T, mem_weight, win_weight)


def solution(mesh):
    return jax.shard_map(
        shards,
        mesh=mesh,
        in_specs=(
            P(("ctx", "mem"), None),
            P(("ctx", "mem"), None),
            P(),
            P("mem", None, None),
            P("mem", None),
        ),
        out_specs=P(("ctx", "mem"), None),
        check_vma=False,
    )
```

time: 410 us -> 173 us (0.42)
  the two profiles are of different devices: /device:TPU:7 before, /device:TPU:28 now
where the time goes in v1:
time: 173 us
  Pallas kernels  172 us (99%)
    pallas_call x1, Pallas kernels, shards(): pl.pallas_call(kernel, out_shape=jax.ShapeDtypeStruct((TOK, WIDTH), bf16)...  172 us

profile of v1, /device:TPU:28, one launch (start us, length us, event | category | flops | bytes accessed | tf_op | source)
XLA Modules:
  0.0 173.2 jit_solution(6639938570168159255)
XLA Ops:
  0.0 171.6 %shard_map.55 = bf16[256,512]{1,0:T(8,128)(2,1)} custom-call(bf16[256,1024]{1,0:T(8,128)(2,1)} %tok.1, s32[2,256]{1,0:T(2,128)} %bitcast.3, bf16[16,1024]{1,0:T(8,128)(2,1)} %bitcast.2, bf16[1,1024,1536]{2,1,0:T(8,128)(2,1)} %w_hbm.1, bf16[64,1536]{1,0:T(8,128)(2,1)} %win.1), custom_call_target="tpu_custom_call" | custom-call | tf_op jit(solution)/shard_map/pallas_call | solution.py:382
  171.6 1.7 copy.7

commit v2 on v1

v2 whole, which is shorter than its diff:
```python
import functools

import jax
import jax.numpy as jnp
from jax import lax
from jax.experimental import pallas as pl
from jax.experimental.pallas import tpu as pltpu
from jax.sharding import PartitionSpec as P

MESH = pl.DeviceIdType.MESH
HEADS = 4
HDIM = 128
WIDTH = HEADS * HDIM
WINDOW = 512
TOK = 256
MEMS = 16
CAP = 48
ROWS = MEMS * CAP
DEPTH = 1024
COLS = 3 * WIDTH
CHIPS = 16
WIN_TILES = COLS // 128
norm_eps = 1e-06
bf16 = jnp.bfloat16
f32 = jnp.float32


def mm(a, b):
    return jnp.dot(a, b, preferred_element_type=f32)


def mm_nt(a, b):
    return lax.dot_general(a, b, (((1,), (1,)), ((), ())), preferred_element_type=f32)


def mm_tn(a, b):
    return lax.dot_general(a, b, (((0,), (0,)), ((), ())), preferred_element_type=f32)


def remote(src, dst, send, recv, device):
    return pltpu.make_async_remote_copy(
        src_ref=src, dst_ref=dst, send_sem=send, recv_sem=recv, device_id=device, device_id_type=MESH
    )


def cols(start, size=128):
    return pl.ds(pl.multiple_of(start, 128), size)


def rows_of(j, size=CAP):
    return pl.ds(pl.multiple_of(j * size, 16), size)


def loop(low, high, body):
    def step(n, carry):
        body(n)
        return carry

    lax.fori_loop(low, high, step, 0)


def kernel(
    tok, routes, router, w_hbm, win, out,
    near, slots_in, pick, pick0, pick1, sbuf, rbuf, wmem, wz, wwin, proj, intra, winq, kv, kvx,
    st_own, st_part, st_send, st_all, pre_send, pre_part, pre, fbuf, ret, wout, gcol, slots,
    s_chain, r_chain, s_slot, r_slot, s_disp, r_disp, r_far, s_ret, r_ret, s_wz, r_wz, s_wp, r_wp, s_st, r_st,
    one_s, one_r, l_ret, local,
):
    ctx = lax.axis_index("ctx")
    me = lax.axis_index("mem")
    chip = ctx // 2
    core = ctx % 2
    seq = ctx * MEMS + me

    def member(j):
        return {"ctx": ctx, "mem": j}

    def peer(j):
        return {"ctx": 2 * j + core, "mem": me}

    def wrap(n):
        return (n + 32) % 16

    partner = {"ctx": 2 * chip + 1 - core, "mem": me}
    after = {"ctx": (ctx + 1) % 32, "mem": me}
    before = {"ctx": (ctx + 31) % 32, "mem": me}

    w_copy = pltpu.make_async_copy(w_hbm.at[0], wmem, local.at[0])
    w_copy.start()

    barrier = pltpu.get_barrier_semaphore()

    def greet(off):
        pl.semaphore_signal(barrier, inc=1, device_id=member(wrap(me + off)), device_id_type=MESH)
        pl.semaphore_signal(barrier, inc=1, device_id=peer(wrap(chip + off)), device_id_type=MESH)

    loop(1, 16, greet)
    for device in (partner, after, before):
        pl.semaphore_signal(barrier, inc=1, device_id=device, device_id_type=MESH)

    first, second = routes[0:1, :], routes[1:2, :]
    mem_ids = lax.broadcasted_iota(jnp.int32, (MEMS, TOK), 0)
    match0 = jnp.where(mem_ids == first, 1.0, 0.0).astype(f32)
    match1 = jnp.where(mem_ids == second, 1.0, 0.0).astype(f32)
    earlier = jnp.where(
        lax.broadcasted_iota(jnp.int32, (TOK, TOK), 0) < lax.broadcasted_iota(jnp.int32, (TOK, TOK), 1), 1.0, 0.0
    ).astype(bf16)
    counts = mm((match0 + match1).astype(bf16), earlier)
    slot0 = jnp.sum(match0 * counts, axis=0, keepdims=True).astype(jnp.int32)
    slot1 = jnp.sum(match1 * counts, axis=0, keepdims=True).astype(jnp.int32)
    slots[0:1, :] = first * CAP + slot0
    slots[1:2, :] = second * CAP + slot1

    def chosen(table, memory, size=CAP, skip=0):
        ids = lax.broadcasted_iota(jnp.int32, (size, TOK), 0) + (memory * CAP + skip)
        return jnp.where((ids == table[0:1, :]) | (ids == table[1:2, :]), 1.0, 0.0).astype(bf16)

    own_pick = chosen(slots, me)
    rbuf[rows_of(me), :] = mm(own_pick, tok[...]).astype(bf16)

    pl.semaphore_wait(barrier, 15 + 15 + 1 + 2)

    ways = (1, -1)

    def chain(d, hop, k):
        part = cols(k * 256, 256)
        src = tok.at[:, part] if hop == 0 else near.at[d, 0, :, part]
        at = (2 * d + hop) * 4 + k
        return remote(src, near.at[d, hop, :, part], s_chain.at[at], r_chain.at[at], member(wrap(me + ways[d])))

    def slot_chain(d, hop):
        src = slots if hop == 0 else slots_in.at[d, 0]
        at = 2 * d + hop
        return remote(src, slots_in.at[d, hop], s_slot.at[at], r_slot.at[at], member(wrap(me + ways[d])))

    for d in range(2):
        slot_chain(d, 0).start()

    def first_hop(k):
        for d in range(2):
            chain(d, 0, k).start()

    loop(0, 4, first_hop)

    half = pl.ds(pl.multiple_of(core * 32, 32), 32)

    def wz_copy(j, slot, device):
        return remote(win.at[half, cols(chip * 128)], wz.at[slot], s_wz.at[j], r_wz.at[slot], device)

    @pl.when(chip < WIN_TILES)
    def _():
        def send(off):
            j = wrap(me + off)
            wz_copy(j, me, member(j)).start()

        loop(1, 16, send)
        pltpu.make_async_copy(win.at[half, cols(chip * 128)], wz.at[me], local.at[1]).start()

    far = (32, 16)

    def disp_copy(d, e, k):
        part = cols(k * 256, 256)
        size = CAP if e < 5 else far[d]
        skip = far[0] if e == 5 and d else 0
        slot = wrap(me - 2 * ways[d])
        target = pl.ds(pl.multiple_of(slot * CAP + skip, 16), size)
        recv = r_far.at[k] if e == 5 and d else r_disp.at[16 * k + slot]
        return remote(
            sbuf.at[d, e * CAP : e * CAP + size, part],
            rbuf.at[target, part],
            s_disp.at[(d * 6 + e) * 4 + k],
            recv,
            member(wrap(me + ways[d] * (1 + e))),
        )

    def second_hop(k):
        for d in range(2):
            chain(d, 0, k).wait_recv()
            chain(d, 1, k).start()

    def relay(k):
        part = cols(k * 256, 256)
        for d in range(2):
            chain(d, 1, k).wait_recv()
            sbuf[d, :, part] = mm(pick[d], near[d, 1, :, part]).astype(bf16)
            for e in range(5, -1, -1):
                disp_copy(d, e, k).start()

    for d in range(2):
        slot_chain(d, 0).wait_recv()
        slot_chain(d, 1).start()
    loop(0, 2, second_hop)
    def wp_block(j, b):
        return wwin.at[:, pl.ds(pl.multiple_of(b * 32, 32), 32), cols(j * 128)]

    @pl.when(chip < WIN_TILES)
    def _():
        def arrive(off):
            j = wrap(me + off)
            wz_copy(j, j, member(j)).wait_recv()

        loop(1, 16, arrive)
        pltpu.make_async_copy(win.at[half, cols(chip * 128)], wz.at[me], local.at[1]).wait()

        def send(off):
            j = wrap(chip + off)
            remote(wz, wp_block(chip, core), s_wp.at[j], r_wp.at[chip], peer(j)).start()

        loop(1, 16, send)
        pltpu.make_async_copy(wz, wp_block(chip, core), local.at[1]).start()

    for d in range(2):
        slot_chain(d, 1).wait_recv()
        for e in range(6):
            size = CAP if e < 5 else far[d]
            skip = far[0] if e == 5 and d else 0
            pick[d, e * CAP : e * CAP + size] = chosen(slots_in[d, 1], wrap(me + ways[d] * (1 + e)), size, skip)
        if d:
            pick[d, 5 * CAP + far[1] : 5 * CAP + far[0]] = jnp.zeros((far[0] - far[1], TOK), bf16)
    relay(0)
    second_hop(2)
    relay(1)
    second_hop(3)
    loop(2, 4, relay)

    for d in range(2):
        for hop in range(2):
            mine = chosen(slots_in[d, hop], me)
            rbuf[rows_of(wrap(me - ways[d] * (hop + 1))), :] = mm(mine, near[d, hop]).astype(bf16)

    logits = mm_nt(router[...], tok[...])
    diff = jnp.sum((match0 - match1) * logits, axis=0, keepdims=True)
    gate = jax.nn.sigmoid(diff)
    gcol[...] = jnp.transpose(jnp.broadcast_to(gate, (128, TOK)))
    row_ids = lax.broadcasted_iota(jnp.int32, (ROWS, TOK), 0)
    pick0[...] = jnp.where(row_ids == slots[0:1, :], 1.0, 0.0).astype(bf16)
    pick1[...] = jnp.where(row_ids == slots[1:2, :], 1.0, 0.0).astype(bf16)

    def wp_arrive(j):
        @pl.when(j != chip)
        def _():
            remote(wz, wp_block(j, core), s_wp.at[j], r_wp.at[j], partner).wait_recv()

        @pl.when(j == chip)
        def _():
            pltpu.make_async_copy(wz, wp_block(j, core), local.at[1]).wait()

    loop(0, WIN_TILES, wp_arrive)
    wc_copy = remote(wwin.at[:, half, :], wwin.at[:, half, :], one_s.at[0], one_r.at[0], partner)
    wc_copy.start()
    wc_copy.wait_recv()

    def win_block(n):
        return wwin[:, :, cols(n * 256, 256)].reshape(DEPTH, 256)

    def win_query(n):
        winq[:, cols(n * 256, 256)] = mm(tok[...], win_block(n)).astype(bf16)

    loop(0, 2, win_query)

    crosses = (me <= 1, me == 0)

    def win_keys(n):
        w = win_block(n + 2)
        at = cols(n * 256, 256)
        kv[2 * TOK : 3 * TOK, at] = mm(tok[...], w).astype(bf16)
        for g in range(2):
            res = mm(near[0, 1 - g], w).astype(bf16)

            @pl.when(crosses[g])
            def _():
                kvx[g * TOK : (g + 1) * TOK, at] = res

            @pl.when(jnp.logical_not(crosses[g]))
            def _():
                kv[g * TOK : (g + 1) * TOK, at] = res

    loop(0, 4, win_keys)

    def kv_copy(g):
        rows = pl.ds(g * TOK, TOK)
        return remote(kvx.at[rows], kv.at[rows], one_s.at[1 + g], one_r.at[1 + g], after)

    for g in range(2):

        @pl.when(crosses[g])
        def _():
            kv_copy(g).start()

    w_copy.wait()

    def arrived(dist, k):
        j = wrap(me - dist)
        part = cols(k * 256, 256)
        return remote(
            rbuf.at[rows_of(j), part], rbuf.at[rows_of(j), part], s_disp.at[0], r_disp.at[16 * k + j], partner
        )

    def half_arrived(d, k):
        j = wrap(me + 8)
        part = cols(k * 256, 256)
        target = pl.ds(pl.multiple_of(j * CAP + (far[0] if d else 0), 16), far[d])
        sem = r_far.at[k] if d else r_disp.at[16 * k + j]
        return remote(rbuf.at[target, part], rbuf.at[target, part], s_disp.at[0], sem, partner)

    def all_arrived(k):
        def one(dist):
            arrived(dist, k).wait_recv()
            arrived(-dist, k).wait_recv()

        loop(3, 8, one)
        half_arrived(0, k).wait_recv()
        half_arrived(1, k).wait_recv()

    loop(0, 4, all_arrived)

    def project(n):
        def tile(g):
            proj[rows_of(g, 256), cols(n * 256, 256)] = mm(rbuf[rows_of(g, 256), :], wmem[:, cols(n * 256, 256)]).astype(
                bf16
            )

        loop(0, 3, tile)

    loop(2, 6, project)

    def state(h):
        st_own[h] = mm_tn(proj[:, cols(WIDTH + h * HDIM)], proj[:, cols(2 * WIDTH + h * HDIM)])

    loop(0, HEADS, state)
    st_copy = remote(st_own, st_part, one_s.at[3], one_r.at[3], partner)
    st_copy.start()
    loop(0, 2, project)
    st_copy.wait()
    mine = pl.ds(2 * core, 2)
    st_send[...] = (st_own[mine] + st_part[mine]).astype(bf16)

    def st_copy_of(j, slot, device):
        return remote(st_send, st_all.at[slot], s_st.at[j], r_st.at[slot], device)

    loop(chip + 1, CHIPS, lambda j: st_copy_of(j, chip, peer(j)).start())

    def attend(h):
        q = proj[:, cols(h * HDIM)]
        k = proj[:, cols(WIDTH + h * HDIM)]
        v = proj[:, cols(2 * WIDTH + h * HDIM)]
        keep = lax.broadcasted_iota(jnp.int32, (256, 256), 1) <= lax.broadcasted_iota(jnp.int32, (256, 256), 0)
        for b in range(3):
            lo, hi = b * 256, (b + 1) * 256
            scores = jnp.where(keep, mm_nt(q[lo:hi], k[lo:hi]), 0.0).astype(bf16)
            total = mm(scores, v[lo:hi])
            if b:
                total = total + mm(mm_nt(q[lo:hi], k[:lo]).astype(bf16), v[:lo])
            intra[lo:hi, cols(h * HDIM)] = total

    loop(0, HEADS, attend)
    pre_send[...] = jnp.zeros_like(pre_send)

    def st_in(j):
        st_copy_of(j, j, partner).wait_recv()
        pre_send[...] += st_all[j].astype(f32)

    loop(0, chip, st_in)
    pre_copy = remote(pre_send, pre_part, one_s.at[4], one_r.at[4], partner)
    pre_copy.start()
    pre_copy.wait_recv()

    for h in range(HEADS):
        lower = core == h // 2

        @pl.when(lower)
        def _():
            st_own[h] = pre_send[h % 2]

        @pl.when(jnp.logical_not(lower))
        def _():
            st_own[h] = pre_part[h % 2]

    @pl.when(core == 0)
    def _():
        pre[...] = st_own[...].astype(bf16)

    @pl.when(core == 1)
    def _():
        pre[...] = (st_own[...] + st_part[...]).astype(bf16)

    def ret_copy(j, slot, n):
        part = cols(n * 256, 256)
        return remote(
            fbuf.at[rows_of(j), part],
            ret.at[rows_of(slot), part],
            s_ret.at[16 * n + j],
            r_ret.at[16 * n + slot],
            member(j),
        )

    def own_ret(n):
        part = cols(n * 256, 256)
        return pltpu.make_async_copy(fbuf.at[rows_of(me), part], ret.at[rows_of(me), part], l_ret.at[n])

    def finish(n):
        for u in range(2):
            at = cols(n * 256 + u * HDIM)
            summed = intra[:, at] + mm(proj[:, at], pre[2 * n + u])
            factor = lax.rsqrt(jnp.mean(summed * summed, axis=-1, keepdims=True) + norm_eps)
            fbuf[:, at] = (summed * factor).astype(bf16)

        def send(m):
            dist = 8 - (m + 1) // 2
            j = wrap(me + jnp.where(m % 2 == 0, dist, MEMS - dist))
            ret_copy(j, me, n).start()

        loop(0, 15, send)
        own_ret(n).start()

    loop(0, 2, finish)

    for g in range(2):

        @pl.when(crosses[g])
        def _():
            kv_copy(g).wait_recv()

    first_pos = seq * TOK

    def window(h):
        for b in range(2):
            lo = b * 128
            q = winq[lo : lo + 128, cols(h * HDIM)]
            k = kv[lo : lo + 640, cols(h * HDIM)]
            v = kv[lo : lo + 640, cols(WIDTH + h * HDIM)]
            scores = mm_nt(q, k) * HDIM ** (-0.5)
            key = lax.broadcasted_iota(jnp.int32, (128, 640), 1)
            distance = lax.broadcasted_iota(jnp.int32, (128, 640), 0) + 2 * TOK - key
            allowed = (distance >= 0) & (distance < WINDOW) & (key + lo + first_pos - 2 * TOK >= 0)
            masked = jnp.where(allowed, scores, -1e30)
            expo = jnp.exp(masked - jnp.max(masked, axis=-1, keepdims=True))
            probs = (expo / jnp.sum(expo, axis=-1, keepdims=True)).astype(bf16)
            wout[lo : lo + 128, cols(h * HDIM)] = mm(probs, v)

    loop(0, HEADS, window)


    def combine(n):
        def ret_in(off):
            j = wrap(me + off)
            ret_copy(j, j, n).wait_recv()

        loop(1, 16, ret_in)
        own_ret(n).wait()
        for u in range(2):
            at = cols(n * 256 + u * HDIM)
            res = ret[:, at]
            g = gcol[...]
            part = g * mm_tn(pick0[...], res) + (1.0 - g) * mm_tn(pick1[...], res)
            out[:, at] = (part + wout[:, at]).astype(bf16)

    loop(0, 2, combine)

    def left(off):
        j = wrap(me + off)
        loop(0, 2, lambda n: ret_copy(j, me, n).wait_send())

        @pl.when(chip < WIN_TILES)
        def _():
            wz_copy(j, me, member(j)).wait_send()
            i = wrap(chip + off)
            remote(wz, wp_block(chip, core), s_wp.at[i], r_wp.at[chip], peer(i)).wait_send()

    loop(1, 16, left)

    def parts_left(k):
        for d in range(2):
            for hop in range(2):
                chain(d, hop, k).wait_send()
            for e in range(6):
                disp_copy(d, e, k).wait_send()

    loop(0, 4, parts_left)
    for d in range(2):
        for hop in range(2):
            slot_chain(d, hop).wait_send()
    for g in range(2):

        @pl.when(crosses[g])
        def _():
            kv_copy(g).wait_send()

    loop(chip + 1, CHIPS, lambda j: st_copy_of(j, chip, peer(j)).wait_send())
    wc_copy.wait_send()
    pre_copy.wait_send()


def shards(tokens, routes, router, mem_weight, win_weight):
    vmem = pl.BlockSpec(memory_space=pltpu.VMEM)
    dma = pltpu.SemaphoreType.DMA
    return pl.pallas_call(
        kernel,
        out_shape=jax.ShapeDtypeStruct((TOK, WIDTH), bf16),
        in_specs=[vmem, vmem, vmem, pl.BlockSpec(memory_space=pl.ANY), vmem],
        out_specs=vmem,
        scratch_shapes=[
            pltpu.VMEM((2, 2, TOK, DEPTH), bf16),
            pltpu.VMEM((2, 2, 2, TOK), jnp.int32),
            pltpu.VMEM((2, 5 * CAP + 32, TOK), bf16),
            pltpu.VMEM((ROWS, TOK), bf16),
            pltpu.VMEM((ROWS, TOK), bf16),
            pltpu.VMEM((2, 5 * CAP + 32, DEPTH), bf16),
            pltpu.VMEM((ROWS, DEPTH), bf16),
            pltpu.VMEM((DEPTH, COLS), bf16),
            pltpu.VMEM((MEMS, 32, 128), bf16),
            pltpu.VMEM((MEMS, 64, COLS), bf16),
            pltpu.VMEM((ROWS, COLS), bf16),
            pltpu.VMEM((ROWS, WIDTH), f32),
            pltpu.VMEM((TOK, WIDTH), bf16),
            pltpu.VMEM((3 * TOK, 2 * WIDTH), bf16),
            pltpu.VMEM((2 * TOK, 2 * WIDTH), bf16),
            pltpu.VMEM((HEADS, HDIM, HDIM), f32),
            pltpu.VMEM((HEADS, HDIM, HDIM), f32),
            pltpu.VMEM((2, HDIM, HDIM), bf16),
            pltpu.VMEM((CHIPS, 2, HDIM, HDIM), bf16),
            pltpu.VMEM((2, HDIM, HDIM), f32),
            pltpu.VMEM((2, HDIM, HDIM), f32),
            pltpu.VMEM((HEADS, HDIM, HDIM), bf16),
            pltpu.VMEM((ROWS, WIDTH), bf16),
            pltpu.VMEM((ROWS, WIDTH), bf16),
            pltpu.VMEM((TOK, WIDTH), f32),
            pltpu.VMEM((TOK, 128), f32),
            pltpu.VMEM((2, TOK), jnp.int32),
        ]
        + [dma((n,)) for n in (16, 16, 4, 4, 48, 64, 4, 32, 32)]
        + [dma((16,))] * 6
        + [dma((5,)), dma((5,)), dma((2,)), dma((2,))],
        compiler_params=pltpu.CompilerParams(
            collective_id=0, has_side_effects=True, vmem_limit_bytes=56 * 1024 * 1024
        ),
    )(tokens, routes.T, router.T, mem_weight, win_weight)


def solution(mesh):
    return jax.shard_map(
        shards,
        mesh=mesh,
        in_specs=(
            P(("ctx", "mem"), None),
            P(("ctx", "mem"), None),
            P(),
            P("mem", None, None),
            P("mem", None),
        ),
        out_specs=P(("ctx", "mem"), None),
        check_vma=False,
    )
```

time: 173 us -> 150 us (0.87)
  the two profiles are of different devices: /device:TPU:28 before, /device:TPU:7 now
where the time goes in v2:
time: 150 us
  Pallas kernels  148 us (99%)
  local copies, waits for them, and re-layouts  1.67 us (1%)
    pallas_call x1, Pallas kernels, shards(): pl.pallas_call(kernel, out_shape=jax.ShapeDtypeStruct((TOK, WIDTH), bf16)...  148 us

profile of v2, /device:TPU:7, one launch (start us, length us, event | category | flops | bytes accessed | tf_op | source)
XLA Modules:
  0.0 149.7 jit_solution(4611449454042333344)
XLA Ops:
  0.0 148.0 %shard_map.55 = bf16[256,512]{1,0:T(8,128)(2,1)} custom-call(bf16[256,1024]{1,0:T(8,128)(2,1)} %tok.1, s32[2,256]{1,0:T(2,128)} %bitcast.3, bf16[16,1024]{1,0:T(8,128)(2,1)} %bitcast.2, bf16[1,1024,1536]{2,1,0:T(8,128)(2,1)} %w_hbm.1, bf16[64,1536]{1,0:T(8,128)(2,1)} %win.1), custom_call_target="tpu_custom_call" | custom-call | tf_op jit(solution)/shard_map/pallas_call | solution.py:497
  148.0 1.7 %copy.7 = bf16[256,512]{1,0:T(8,128)(2,1)} copy(bf16[256,512]{1,0:T(8,128)(2,1)} %shard_map.55) | data formatting | bytes 524288
